TPU v7x, 32 devices: a whole 2x2x4 slice. The times are simulated.
32 devices in a mesh: dp: 2 (over x), expert: 16 (over z, y, core).
Axes of the slice: x: 2, y: 2, z: 4, core: 2. Of those that a mesh axis runs over, the one named last changes fastest.
Arguments:
- tokens: bfloat16 [4096, 1024], P(('dp', 'expert')), may hold values from -6 to 6
- cotangent: bfloat16 [4096, 1024], P(('dp', 'expert')), may hold values from -6 to 6
- expert_ids: int32 [4096, 6], P(('dp', 'expert')), may hold values from 0 to 15, all different within a row; in each aligned block of 128 rows (0 to 127, 128 to 255, ...) at most 60 rows name the same one
- gate_weights: float32 [4096, 6], P(('dp', 'expert')), may hold values from 0.05 to 0.3
- partner: int32 [16], replicated, may hold values from 0 to 15, as said below
- weights: bfloat16 [16, 1024, 3, 384], P('expert', 'dp'), may hold values from -0.3125 to 0.3125
- first_moment: bfloat16 [16, 1024, 3, 384], P('expert', 'dp'), may hold values from -6 to 6
- second_moment: bfloat16 [16, 1024, 3, 384], P('expert', 'dp'), may hold values from 0.099609375 to 4
Outputs:
- mixed: bfloat16 [4096, 1024], P(('dp', 'expert'))
- token_grad: bfloat16 [4096, 1024], P(('dp', 'expert'))
- new_weights: bfloat16 [16, 1024, 3, 384], P('expert', 'dp')
- new_first: bfloat16 [16, 1024, 3, 384], P('expert', 'dp')
- new_second: bfloat16 [16, 1024, 3, 384], P('expert', 'dp')
Inputs may be any that keep to these rules, and one draw needn't show every extreme that they name: `expert_ids`: each row names 6 different experts. Among the 128 tokens of one device (aligned blocks of rows), no expert is named by more than 60 tokens, and in every draw some block names some expert exactly 60 times. partner[partner[h]] = h and partner[h] != h for every h.
All inputs are finite; a program needn't handle non-finite values.
Results may differ from a plain program's by a relative error of at most 0.024.
Values may be sent and summed in bfloat16 or wider, within the bound.
A program may use at most 64 MiB of HBM per device.

v0:
```python
import jax
import jax.numpy as jnp
from jax import lax
from jax.sharding import PartitionSpec as P

beta_one = 0.9
beta_two = 0.95
learn_rate = 0.01
decay_rate = 0.1
eps_adam = 1e-08
step_count = 100


def send_rows(parts):
    return (lax.all_to_all(parts[0], "expert", split_axis=0, concat_axis=0, tiled=True),)


def send_back(parts):
    return (lax.all_to_all(parts[0], "expert", split_axis=0, concat_axis=0, tiled=True),)


def shards_by_slot(
    tokens, cotangent, expert_ids, gate_weights, partner, weights, first_moment, second_moment
):
    experts_here = lax.axis_size("expert")
    tok_dev, model_width = tokens.shape
    top_count = expert_ids.shape[1]
    hidden_width = weights.shape[3]
    capacity = min(tok_dev, max(2, 5 * tok_dev * top_count // (4 * experts_here)))
    item_total = tok_dev * top_count
    slot_total = experts_here * capacity
    flat_ids = expert_ids.reshape(item_total)
    onehot = (flat_ids[:, None] == jnp.arange(experts_here, dtype=jnp.int32)[None, :]).astype(
        jnp.int32
    )
    before = jnp.cumsum(onehot, axis=0) - onehot
    slot_of = jnp.sum(before * onehot, axis=1)
    position = flat_ids * capacity + slot_of
    source = (
        jnp.full((slot_total,), item_total, jnp.int32)
        .at[position]
        .set(jnp.arange(item_total, dtype=jnp.int32))
    )
    token_of = source // top_count
    zero_row = jnp.zeros((1, model_width), jnp.bfloat16)
    x_send = jnp.concatenate([tokens, zero_row], axis=0)[token_of].reshape(
        experts_here, capacity, model_width
    )
    gate_flat = gate_weights.reshape(item_total)
    gate_pad = jnp.concatenate([gate_flat, jnp.zeros((1,), jnp.float32)])
    cot_rows = jnp.concatenate([cotangent, zero_row], axis=0)[token_of].astype(jnp.float32)
    dy_send = (
        (gate_pad[source][:, None] * cot_rows)
        .astype(jnp.bfloat16)
        .reshape(experts_here, capacity, model_width)
    )
    gathered = lax.all_gather(weights, "dp", axis=1, tiled=True)[0]
    gate_up = gathered[:, 0:2, :].reshape(model_width, 2 * hidden_width)
    down_proj = gathered[:, 2, :]
    block_shape = (experts_here, capacity, model_width)
    (x_recv,) = send_rows((x_send,))
    forward_x_rows = x_recv.reshape(slot_total, model_width)
    both_proj = jnp.dot(forward_x_rows, gate_up, preferred_element_type=jnp.float32)
    pre_act = both_proj[:, :hidden_width]
    lin_act = both_proj[:, hidden_width:]
    sigmoid_pre = jax.nn.sigmoid(pre_act)
    silu_pre = pre_act * sigmoid_pre
    forward_hidden = (silu_pre * lin_act).astype(jnp.bfloat16)
    out_rows = jnp.dot(forward_hidden, down_proj.T, preferred_element_type=jnp.float32).astype(
        jnp.bfloat16
    )
    x_rows, saved, hidden, out_rows = (
        forward_x_rows,
        (pre_act, lin_act, sigmoid_pre, silu_pre),
        forward_hidden,
        out_rows,
    )
    (out_back,) = send_back((out_rows.reshape(block_shape),))
    (dy_recv,) = send_rows((dy_send,))
    pre_act, lin_act, sigmoid_pre, silu_pre = saved
    backward_dy_rows = dy_recv.reshape(slot_total, model_width)
    hidden_grad = jnp.dot(backward_dy_rows, down_proj, preferred_element_type=jnp.float32)
    pre_grad = (hidden_grad * lin_act * sigmoid_pre * (1.0 + pre_act * (1.0 - sigmoid_pre))).astype(
        jnp.bfloat16
    )
    lin_grad = (hidden_grad * silu_pre).astype(jnp.bfloat16)
    backward_both_grad = jnp.concatenate([pre_grad, lin_grad], axis=1)
    item_grad = jnp.dot(backward_both_grad, gate_up.T, preferred_element_type=jnp.float32).astype(
        jnp.bfloat16
    )
    dy_rows, both_grad, item_grad = (backward_dy_rows, backward_both_grad, item_grad)
    (grad_back,) = send_back((item_grad.reshape(block_shape),))
    out_items = (
        out_back.reshape(slot_total, model_width)[position].astype(jnp.float32) * gate_flat[:, None]
    )
    mixed = jnp.sum(out_items.reshape(tok_dev, top_count, model_width), axis=1).astype(jnp.bfloat16)
    grad_items = grad_back.reshape(slot_total, model_width)[position].astype(jnp.float32)
    token_grad = jnp.sum(grad_items.reshape(tok_dev, top_count, model_width), axis=1).astype(
        jnp.bfloat16
    )
    count = lax.axis_size("dp") * weights.shape[1]
    proj_grad = jnp.dot(x_rows.T, both_grad, preferred_element_type=jnp.float32)
    down_grad = jnp.dot(dy_rows.T, hidden, preferred_element_type=jnp.float32)
    grad_sum = lax.psum_scatter(
        jnp.concatenate(
            [proj_grad.reshape(count, 2, hidden_width), down_grad.reshape(count, 1, hidden_width)],
            axis=1,
        ).astype(jnp.bfloat16),
        "dp",
        scatter_dimension=0,
        tiled=True,
    ).astype(jnp.float32)
    w_old = weights[0].astype(jnp.float32)
    m_old = first_moment[0].astype(jnp.float32)
    v_old = second_moment[0].astype(jnp.float32)
    m_new = beta_one * m_old + (1.0 - beta_one) * grad_sum
    v_new = beta_two * v_old + (1.0 - beta_two) * grad_sum * grad_sum
    m_hat = m_new / (1.0 - beta_one**step_count)
    v_hat = v_new / (1.0 - beta_two**step_count)
    w_new = w_old - learn_rate * (m_hat / (jnp.sqrt(v_hat) + eps_adam) + decay_rate * w_old)
    pieces = (
        w_new.astype(jnp.bfloat16).reshape(experts_here, -1),
        m_new.astype(jnp.bfloat16).reshape(experts_here, -1),
        v_new.astype(jnp.bfloat16).reshape(experts_here, -1),
    )
    spread = (
        lax.all_to_all(pieces[0], "expert", split_axis=0, concat_axis=0, tiled=True),
        lax.all_to_all(pieces[1], "expert", split_axis=0, concat_axis=0, tiled=True),
        lax.all_to_all(pieces[2], "expert", split_axis=0, concat_axis=0, tiled=True),
    )
    ordered = (spread[0][partner], spread[1][partner], spread[2][partner])
    homed = (
        lax.all_to_all(ordered[0], "expert", split_axis=0, concat_axis=0, tiled=True),
        lax.all_to_all(ordered[1], "expert", split_axis=0, concat_axis=0, tiled=True),
        lax.all_to_all(ordered[2], "expert", split_axis=0, concat_axis=0, tiled=True),
    )
    new_weights = homed[0].reshape(weights.shape)
    new_first = homed[1].reshape(weights.shape)
    new_second = homed[2].reshape(weights.shape)
    return (mixed, token_grad, new_weights, new_first, new_second)


def adam(w_old, m_old, v_old, grad_sum):
    m_new = beta_one * m_old + (1.0 - beta_one) * grad_sum
    v_new = beta_two * v_old + (1.0 - beta_two) * grad_sum * grad_sum
    m_hat = m_new / (1.0 - beta_one**step_count)
    v_hat = v_new / (1.0 - beta_two**step_count)
    w_new = w_old - learn_rate * (m_hat / (jnp.sqrt(v_hat) + eps_adam) + decay_rate * w_old)
    return (w_new, m_new, v_new)


def shards_dense(
    tokens, cotangent, expert_ids, gate_weights, partner, weights, first_moment, second_moment
):
    experts_here = lax.axis_size("expert")
    me = lax.axis_index("expert")
    tok_dev, model_width = tokens.shape
    own_rows, hidden_width = (weights.shape[1], weights.shape[3])
    width = 3 * hidden_width
    f32, bf16 = (jnp.float32, jnp.bfloat16)
    hits = expert_ids[:, :, None] == jnp.arange(experts_here, dtype=jnp.int32)[None, None, :]
    gate_table = jnp.sum(jnp.where(hits, gate_weights[:, :, None], 0.0), axis=1).T
    w_flat = weights[0].reshape(own_rows, width)
    gathered = lax.all_gather(w_flat, "dp", axis=0, tiled=True)
    x_rows = lax.all_gather(tokens, "expert", axis=0, tiled=True)
    cot_rows = lax.all_gather(cotangent, "expert", axis=0, tiled=True)
    gate_all = lax.all_gather(gate_table, "expert", axis=0)
    gate = lax.dynamic_index_in_dim(gate_all, me, 1, keepdims=False)
    gate = gate.reshape(experts_here * tok_dev, 1)
    gate_up = gathered[:, : 2 * hidden_width]
    down_proj = gathered[:, 2 * hidden_width :]
    both_proj = jnp.dot(x_rows, gate_up, preferred_element_type=f32)
    pre_act = both_proj[:, :hidden_width]
    lin_act = both_proj[:, hidden_width:]
    sigmoid_pre = jax.nn.sigmoid(pre_act)
    silu_pre = pre_act * sigmoid_pre
    hidden = (silu_pre * lin_act).astype(bf16)
    out_rows = jnp.dot(hidden, down_proj.T, preferred_element_type=f32)
    mixed = lax.psum_scatter(
        (gate * out_rows).astype(bf16), "expert", scatter_dimension=0, tiled=True
    )
    dy_rows = (gate * cot_rows.astype(f32)).astype(bf16)
    hidden_grad = jnp.dot(dy_rows, down_proj, preferred_element_type=f32)
    pre_grad = hidden_grad * lin_act * sigmoid_pre * (1.0 + pre_act * (1.0 - sigmoid_pre))
    lin_grad = hidden_grad * silu_pre
    both_grad = jnp.concatenate([pre_grad.astype(bf16), lin_grad.astype(bf16)], axis=1)
    proj_grad = jnp.dot(x_rows.T, both_grad, preferred_element_type=f32)
    down_grad = jnp.dot(dy_rows.T, hidden, preferred_element_type=f32)
    partial = jnp.concatenate([proj_grad.astype(bf16), down_grad.astype(bf16)], axis=1)
    grad_sum = lax.psum_scatter(partial, "dp", scatter_dimension=0, tiled=True).astype(f32)
    item_grad = jnp.dot(both_grad, gate_up.T, preferred_element_type=f32).astype(bf16)
    token_grad = lax.psum_scatter(item_grad, "expert", scatter_dimension=0, tiled=True)
    m_flat = first_moment[0].reshape(own_rows, width)
    v_flat = second_moment[0].reshape(own_rows, width)
    new_state = adam(w_flat.astype(f32), m_flat.astype(f32), v_flat.astype(f32), grad_sum)
    share = own_rows // experts_here
    outs = []
    for part in new_state:
        pieces = part.astype(bf16).reshape(experts_here, share, width)
        spread = lax.all_to_all(pieces, "expert", split_axis=0, concat_axis=0, tiled=True)
        homed = lax.all_to_all(spread[partner], "expert", split_axis=0, concat_axis=0, tiled=True)
        outs.append(homed.reshape(weights.shape))
    return (mixed, token_grad, *outs)


def shards(*args):
    replica_rows = lax.axis_size("expert") * args[0].shape[0]
    if replica_rows <= 4096 and args[5].shape[1] % (16 * lax.axis_size("expert")) == 0:
        return shards_dense(*args)
    return shards_by_slot(*args)


def solution(mesh):
    in_specs = (
        P(("dp", "expert"), None),
        P(("dp", "expert"), None),
        P(("dp", "expert"), None),
        P(("dp", "expert"), None),
        P(),
        P("expert", "dp", None, None),
        P("expert", "dp", None, None),
        P("expert", "dp", None, None),
    )
    out_specs = (
        P(("dp", "expert"), None),
        P(("dp", "expert"), None),
        P("expert", "dp", None, None),
        P("expert", "dp", None, None),
        P("expert", "dp", None, None),
    )
    return jax.shard_map(shards, mesh=mesh, in_specs=in_specs, out_specs=out_specs, check_vma=False)
```

profile of v0, /device:TPU:15, one launch (start us, length us, event | category | flops | bytes accessed | tf_op | source)
XLA Modules:
  0.0 465.4 jit_solution(3843170583067933573)
XLA Ops:
  7.2 2.4 copy.29
  11.2 16.0 %all-gather = f32[256,128]{1,0:T(8,128)S(1)} all-gather(f32[16,128]{1,0:T(8,128)S(1)} %bitcast.29), channel_id=2, replica_groups=mesh['dp'=2,'expert'=16] {'expert'}, dimensions={0}, use_global_device_ids=true | all-gather | bytes 139264 | tf_op jit(solution)/shard_map/all_gather | solution.py:167
  27.2 19.2 %all-gather.7.cloned.1.call-done = bf16[1024,1152]{0,1:T(8,128)(2,1)} async-done(((bf16[512,1152]{0,1:T(8,128)(2,1)}), bf16[1024,1152]{0,1:T(8,128)(2,1)}) %all-gather.7.cloned.1.call-update) | async-done | bytes 2359312 | tf_op jit(solution)/shard_map/all_gather | solution.py:164
  46.4 53.2 %all-gather.5.cloned.1.call-done = bf16[2048,1024]{1,0:T(8,128)(2,1)} async-done(((bf16[128,1024]{1,0:T(8,128)(2,1)}), bf16[2048,1024]{1,0:T(8,128)(2,1)}) %all-gather.5.cloned.1.call-update) | async-done | bytes 4194320 | tf_op jit(solution)/shard_map/all_gather | solution.py:165
  99.6 8.7 %fusion.14 = f32[2048,768]{0,1:T(8,128)} fusion(bf16[2048,1024]{1,0:T(8,128)(2,1)} %all-gather.5.cloned.1.call-done, bf16[1024,1152]{0,1:T(8,128)(2,1)} %all-gather.7.cloned.1.call-done), kind=kOutput, calls=%fused_computation.32 | convolution fusion | flops 3221225472 | bytes 12058624 | tf_op jit(solution)/shard_map/dot_general | solution.py:172
  108.4 42.5 %all-gather.9.cloned.1.call-done = bf16[2048,1024]{1,0:T(8,128)(2,1)} async-done(((bf16[128,1024]{1,0:T(8,128)(2,1)}), bf16[2048,1024]{1,0:T(8,128)(2,1)}) %all-gather.9.cloned.1.call-update) | async-done | bytes 4194320 | tf_op jit(solution)/shard_map/all_gather | solution.py:166
  150.9 7.5 %multiply_convert_fusion.3 = (bf16[2048,384]{0,1:T(8,128)(2,1)S(1)}, bf16[2048,384]{0,1:T(8,128)(2,1)S(1)}, bf16[2048,384]{0,1:T(8,128)(2,1)S(1)}) fusion(f32[2048,768]{0,1:T(8,128)} %fusion.14, bf16[1024,1152]{0,1:T(8,128)(2,1)} %all-gather.7.cloned.1.call-done, bf16[2048,1024]{1,0:T(8,128)(2,1)} %all-gather.9.cloned.1.call-done, f32[2048]{0:T(1024)S(1)} %bitcast.30), kind=kOutput, calls=%fused_computation.9 | convolution fusion | flops 1628700672 | bytes 15998976 | tf_op jit(solution)/shard_map/dot_general | solution.py:183
  162.2 3.4 fusion.10
  174.6 25.7 %reduce-scatter.8.cloned.1.call-done = bf16[512,1152]{0,1:T(8,128)(2,1)} async-done(((bf16[1024,1152]{0,1:T(8,128)(2,1)}), bf16[512,1152]{0,1:T(8,128)(2,1)}) %reduce-scatter.8.cloned.1.call-update) | async-done | bytes 1179664 | tf_op jit(solution)/shard_map/reduce_scatter | solution.py:190
  200.3 5.8 %fusion.16 = (bf16[512,1152]{0,1:T(8,128)(2,1)S(1)}, bf16[512,1152]{0,1:T(8,128)(2,1)}, bf16[512,1152]{0,1:T(8,128)(2,1)S(1)}) fusion(bf16[512,1152]{0,1:T(8,128)(2,1)} %reduce-scatter.8.cloned.1.call-done, f32[1,512,3,384]{1,3,2,0:T(8,128)} %copy.31, f32[1,512,3,384]{1,3,2,0:T(8,128)} %copy.30, bf16[1,512,3,384]{1,3,2,0:T(8,128)(2,1)S(1)} %copy-done), kind=kLoop, calls=%fused_computation.34 | loop fusion | flops 10616832 | bytes 10616832 | tf_op jit(solution)/shard_map/convert_element_type | solution.py:199
  208.5 6.4 %all-to-all-start = ((bf16[16,32,1152]{2,1,0:T(8,128)(2,1)}), bf16[16,32,1152]{2,1,0:T(8,128)(2,1)S(1)}, u32[]{:S(2)}, u32[]{:S(2)}) async-start(bf16[16,32,1152]{2,1,0:T(8,128)(2,1)} %bitcast.7), calls=%async_computation.3 | async-start | bytes 2359296 | tf_op jit(solution)/shard_map/all_to_all | solution.py:200
  214.9 7.8 %convolution_convert_fusion = bf16[2048,1024]{1,0:T(8,128)(2,1)} fusion(bf16[2048,384]{0,1:T(8,128)(2,1)} %copy-done.11, bf16[2048,384]{0,1:T(8,128)(2,1)} %copy-done.10, bf16[1024,1152]{0,1:T(8,128)(2,1)} %all-gather.7.cloned.1.call-done), kind=kOutput, calls=%fused_computation.5 | convolution fusion | flops 3229614080 | bytes 8912896 | tf_op jit(solution)/shard_map/dot_general | solution.py:191
  224.1 18.5 %all-to-all-done = bf16[16,32,1152]{2,1,0:T(8,128)(2,1)S(1)} async-done(((bf16[16,32,1152]{2,1,0:T(8,128)(2,1)}), bf16[16,32,1152]{2,1,0:T(8,128)(2,1)S(1)}, u32[]{:S(2)}, u32[]{:S(2)}) %all-to-all-start) | async-done | bytes 1179680 | tf_op jit(solution)/shard_map/all_to_all | solution.py:200
  242.6 4.9 %all-to-all-start.2 = ((bf16[16,32,1152]{2,1,0:T(8,128)(2,1)}), bf16[16,32,1152]{2,1,0:T(8,128)(2,1)S(1)}, u32[]{:S(2)}, u32[]{:S(2)}) async-start(bf16[16,32,1152]{2,1,0:T(8,128)(2,1)} %bitcast.8), calls=%async_computation.5 | async-start | bytes 2359296 | tf_op jit(solution)/shard_map/all_to_all | solution.py:200
  248.9 43.1 %all-to-all-done.2 = bf16[16,32,1152]{2,1,0:T(8,128)(2,1)S(1)} async-done(((bf16[16,32,1152]{2,1,0:T(8,128)(2,1)}), bf16[16,32,1152]{2,1,0:T(8,128)(2,1)S(1)}, u32[]{:S(2)}, u32[]{:S(2)}) %all-to-all-start.2) | async-done | bytes 1179680 | tf_op jit(solution)/shard_map/all_to_all | solution.py:200
  292.1 4.9 %all-to-all-start.4 = ((bf16[16,32,1152]{2,1,0:T(8,128)(2,1)}), bf16[16,32,1152]{2,1,0:T(8,128)(2,1)S(1)}, u32[]{:S(2)}, u32[]{:S(2)}) async-start(bf16[16,32,1152]{2,1,0:T(8,128)(2,1)} %bitcast.27), calls=%async_computation.7 | async-start | bytes 2359296 | tf_op jit(solution)/shard_map/all_to_all | solution.py:200
  298.6 33.8 %all-to-all-done.4 = bf16[16,32,1152]{2,1,0:T(8,128)(2,1)S(1)} async-done(((bf16[16,32,1152]{2,1,0:T(8,128)(2,1)}), bf16[16,32,1152]{2,1,0:T(8,128)(2,1)S(1)}, u32[]{:S(2)}, u32[]{:S(2)}) %all-to-all-start.4) | async-done | bytes 1179680 | tf_op jit(solution)/shard_map/all_to_all | solution.py:200
  332.4 5.1 %all-to-all-start.1 = ((bf16[16,32,1152]{2,1,0:T(8,128)(2,1)}), bf16[16,32,1152]{2,1,0:T(8,128)(2,1)S(1)}, u32[]{:S(2)}, u32[]{:S(2)}) async-start(bf16[16,32,1152]{2,1,0:T(8,128)(2,1)} %gather_fusion), calls=%async_computation.4 | async-start | bytes 2359296 | tf_op jit(solution)/shard_map/all_to_all | solution.py:201
  337.5 6.0 %multiply_convert_fusion.1 = bf16[2048,1024]{1,0:T(8,128)(2,1)} fusion(bf16[2048,384]{0,1:T(8,128)(2,1)} %copy-done.9, f32[2048]{0:T(1024)S(1)} %bitcast.32, bf16[1024,1152]{0,1:T(8,128)(2,1)} %all-gather.7.cloned.1.call-done), kind=kOutput, calls=%fused_computation.4 | convolution fusion | flops 1614807040 | bytes 6561792 | tf_op jit(solution)/shard_map/dot_general | solution.py:178
  345.2 20.0 %all-to-all-done.1 = bf16[16,32,1152]{2,1,0:T(8,128)(2,1)S(1)} async-done(((bf16[16,32,1152]{2,1,0:T(8,128)(2,1)}), bf16[16,32,1152]{2,1,0:T(8,128)(2,1)S(1)}, u32[]{:S(2)}, u32[]{:S(2)}) %all-to-all-start.1) | async-done | bytes 1179680 | tf_op jit(solution)/shard_map/all_to_all | solution.py:201
  365.2 4.9 %all-to-all-start.3 = ((bf16[16,32,1152]{2,1,0:T(8,128)(2,1)}), bf16[16,32,1152]{2,1,0:T(8,128)(2,1)}, u32[]{:S(2)}, u32[]{:S(2)}) async-start(bf16[16,32,1152]{2,1,0:T(8,128)(2,1)} %gather_fusion.1), calls=%async_computation.6 | async-start | bytes 2359296 | tf_op jit(solution)/shard_map/all_to_all | solution.py:201
  371.8 43.0 %all-to-all-done.3 = bf16[16,32,1152]{2,1,0:T(8,128)(2,1)} async-done(((bf16[16,32,1152]{2,1,0:T(8,128)(2,1)}), bf16[16,32,1152]{2,1,0:T(8,128)(2,1)}, u32[]{:S(2)}, u32[]{:S(2)}) %all-to-all-start.3) | async-done | bytes 1179680 | tf_op jit(solution)/shard_map/all_to_all | solution.py:201
  414.8 5.0 %all-to-all-start.5 = ((bf16[16,32,1152]{2,1,0:T(8,128)(2,1)}), bf16[16,32,1152]{2,1,0:T(8,128)(2,1)}, u32[]{:S(2)}, u32[]{:S(2)}) async-start(bf16[16,32,1152]{2,1,0:T(8,128)(2,1)} %gather_fusion.2), calls=%async_computation.8 | async-start | bytes 2359296 | tf_op jit(solution)/shard_map/all_to_all | solution.py:201
  424.7 30.4 %all-to-all-done.5 = bf16[16,32,1152]{2,1,0:T(8,128)(2,1)} async-done(((bf16[16,32,1152]{2,1,0:T(8,128)(2,1)}), bf16[16,32,1152]{2,1,0:T(8,128)(2,1)}, u32[]{:S(2)}, u32[]{:S(2)}) %all-to-all-start.5) | async-done | bytes 1179680 | tf_op jit(solution)/shard_map/all_to_all | solution.py:201
  (60 shorter events, 33.0 us)
Async XLA Ops:
  7.2 4.0 copy-start.5
  7.2 4.0 copy-start.4
  7.2 39.2 %all-gather.7.cloned.1.call-start = ((), (), s32[]{:S(2)}) async-start(), calls=%async_computation.10 | async-start | bytes 3538944 | tf_op jit(solution)/shard_map/all_gather | solution.py:164
  9.6 90.0 %all-gather.5.cloned.1.call-start = ((), (), s32[]{:S(2)}) async-start(), calls=%async_computation.9 | async-start | bytes 4456448 | tf_op jit(solution)/shard_map/all_gather | solution.py:165
  10.4 140.5 %all-gather.9.cloned.1.call-start = ((), (), s32[]{:S(2)}) async-start(), calls=%async_computation.12 | async-start | bytes 4456448 | tf_op jit(solution)/shard_map/all_gather | solution.py:166
  11.1 189.2 %reduce-scatter.8.cloned.1.call-start = ((), (), s32[]{:S(2)}) async-start(), calls=%async_computation.14 | async-start | bytes 3538944 | tf_op jit(solution)/shard_map/reduce_scatter | solution.py:190
  150.9 7.5 %copy-start.7 = (bf16[2048,1024]{1,0:T(8,128)(2,1)S(1)}, bf16[2048,1024]{1,0:T(8,128)(2,1)}, u32[]{:S(2)}) copy-start(bf16[2048,1024]{1,0:T(8,128)(2,1)} %all-gather.9.cloned.1.call-done) | copy-start | bytes 12582916
  158.3 2.0 copy-start.9
  158.3 2.0 copy-start.10
  158.4 2.4 copy-start.11
  158.4 3.9 copy-start.6
  167.3 1.3 copy-start.3
  172.6 27.7 %copy-start = (bf16[1,512,3,384]{1,3,2,0:T(8,128)(2,1)S(1)}, bf16[1,512,3,384]{1,3,2,0:T(8,128)(2,1)}, u32[]{:S(2)}) copy-start(bf16[1,512,3,384]{1,3,2,0:T(8,128)(2,1)} %copy.29) | copy-start | bytes 3538948
  208.5 34.1 %all-to-all-start = ((bf16[16,32,1152]{2,1,0:T(8,128)(2,1)}), bf16[16,32,1152]{2,1,0:T(8,128)(2,1)S(1)}, u32[]{:S(2)}, u32[]{:S(2)}) async-start(bf16[16,32,1152]{2,1,0:T(8,128)(2,1)} %bitcast.7), calls=%async_computation.3 | async-start | bytes 2359296 | tf_op jit(solution)/shard_map/all_to_all | solution.py:200
  214.9 243.7 %reduce-scatter.6.cloned.1.call-start = ((), (), s32[]{:S(2)}) async-start(), calls=%async_computation.13 | async-start | bytes 4456448 | tf_op jit(solution)/shard_map/reduce_scatter | solution.py:192
  242.6 49.4 %all-to-all-start.2 = ((bf16[16,32,1152]{2,1,0:T(8,128)(2,1)}), bf16[16,32,1152]{2,1,0:T(8,128)(2,1)S(1)}, u32[]{:S(2)}, u32[]{:S(2)}) async-start(bf16[16,32,1152]{2,1,0:T(8,128)(2,1)} %bitcast.8), calls=%async_computation.5 | async-start | bytes 2359296 | tf_op jit(solution)/shard_map/all_to_all | solution.py:200
  247.5 49.4 %copy-start.8 = (s32[16]{0:T(128)S(1)}, s32[16]{0:T(128)}, u32[]{:S(2)}) copy-start(s32[16]{0:T(128)} %param.12) | copy-start | bytes 196
  292.1 40.4 %all-to-all-start.4 = ((bf16[16,32,1152]{2,1,0:T(8,128)(2,1)}), bf16[16,32,1152]{2,1,0:T(8,128)(2,1)S(1)}, u32[]{:S(2)}, u32[]{:S(2)}) async-start(bf16[16,32,1152]{2,1,0:T(8,128)(2,1)} %bitcast.27), calls=%async_computation.7 | async-start | bytes 2359296 | tf_op jit(solution)/shard_map/all_to_all | solution.py:200
  332.4 32.8 %all-to-all-start.1 = ((bf16[16,32,1152]{2,1,0:T(8,128)(2,1)}), bf16[16,32,1152]{2,1,0:T(8,128)(2,1)S(1)}, u32[]{:S(2)}, u32[]{:S(2)}) async-start(bf16[16,32,1152]{2,1,0:T(8,128)(2,1)} %gather_fusion), calls=%async_computation.4 | async-start | bytes 2359296 | tf_op jit(solution)/shard_map/all_to_all | solution.py:201
  337.5 121.1 %reduce-scatter.4.cloned.1.call-start = ((), (), s32[]{:S(2)}) async-start(), calls=%async_computation.11 | async-start | bytes 4456448 | tf_op jit(solution)/shard_map/reduce_scatter | solution.py:179
  365.2 6.6 %copy-start.1 = (bf16[16,32,1152]{2,1,0:T(8,128)(2,1)}, bf16[16,32,1152]{2,1,0:T(8,128)(2,1)S(1)}, u32[]{:S(2)}) copy-start(bf16[16,32,1152]{2,1,0:T(8,128)(2,1)S(1)} %all-to-all-done.1) | copy-start | bytes 3538948
  365.2 49.5 %all-to-all-start.3 = ((bf16[16,32,1152]{2,1,0:T(8,128)(2,1)}), bf16[16,32,1152]{2,1,0:T(8,128)(2,1)}, u32[]{:S(2)}, u32[]{:S(2)}) async-start(bf16[16,32,1152]{2,1,0:T(8,128)(2,1)} %gather_fusion.1), calls=%async_computation.6 | async-start | bytes 2359296 | tf_op jit(solution)/shard_map/all_to_all | solution.py:201
  414.8 5.0 %copy-start.2 = (bf16[16,32,1152]{2,1,0:T(8,128)(2,1)S(1)}, bf16[16,32,1152]{2,1,0:T(8,128)(2,1)}, u32[]{:S(2)}) copy-start(bf16[16,32,1152]{2,1,0:T(8,128)(2,1)} %copy-done.1) | copy-start | bytes 3538948
  414.8 40.4 %all-to-all-start.5 = ((bf16[16,32,1152]{2,1,0:T(8,128)(2,1)}), bf16[16,32,1152]{2,1,0:T(8,128)(2,1)}, u32[]{:S(2)}, u32[]{:S(2)}) async-start(bf16[16,32,1152]{2,1,0:T(8,128)(2,1)} %gather_fusion.2), calls=%async_computation.8 | async-start | bytes 2359296 | tf_op jit(solution)/shard_map/all_to_all | solution.py:201
Sparse Core Ops, SparseCore 0:
  10.1 36.2 all-gather.6
  48.6 50.9 all-gather.4
  101.8 49.0 all-gather.8
  167.5 32.7 reduce-scatter.7
  222.9 95.5 reduce-scatter.5
  343.7 96.6 reduce-scatter.3
where the time goes:
time: 466 us; the launch traced here: 465 us
  waiting for transfers between devices  331 us (71%)
  matrix products  35.4 us (8%)
  starting transfers between devices  31.2 us (7%)
  local copies, waits for them, and re-layouts  28.5 us (6%)
  blocking collectives  16 us (3%)
  between operations  14.3 us (3%)
  other arithmetic  9.17 us (2%)
    all_to_all x3, waiting for transfers between devices, shards_dense(): lax.all_to_all(pieces, 'expert', split_axis=0, concat_axis=0, tiled=True)  95.4 us
    all_to_all x3, waiting for transfers between devices, shards_dense(): lax.all_to_all(spread[partner], 'expert', split_axis=0, concat_axis=0, ti...  93.4 us
    all_gather x1, waiting for transfers between devices, shards_dense(): x_rows = lax.all_gather(tokens, 'expert', axis=0, tiled=True)  53.2 us
    all_gather x1, waiting for transfers between devices, shards_dense(): cot_rows = lax.all_gather(cotangent, 'expert', axis=0, tiled=True)  42.5 us
    reduce_scatter x1, waiting for transfers between devices, shards_dense(): lax.psum_scatter(partial, 'dp', scatter_dimension=0, tiled=True).astype(f32)  25.7 us
    all_gather x1, waiting for transfers between devices, shards_dense(): gathered = lax.all_gather(w_flat, 'dp', axis=0, tiled=True)  19.2 us
    all_to_all x3, starting transfers between devices, shards_dense(): lax.all_to_all(pieces, 'expert', split_axis=0, concat_axis=0, tiled=True)  16.1 us
    all_gather x1, blocking collectives, shards_dense(): gate_all = lax.all_gather(gate_table, 'expert', axis=0)  16 us
  transfers between devices with their start and end apart: 12, of which 10 were waited for; matrix products, arithmetic and copies ran while one was open for 10% of the time, Pallas kernels for 0%

commit v1 on v0

--- a/solution.py
+++ b/solution.py
@@ -9,6 +9,17 @@
 decay_rate = 0.1
 eps_adam = 1e-08
 step_count = 100
+
+
+def split_up(x, dim, count):
+    before, after = (x.shape[:dim], x.shape[dim + 1 :])
+    return jnp.moveaxis(x.reshape(*before, count, -1, *after), dim, 0)
+
+
+def in_order(blocks, dim):
+    blocks = jnp.moveaxis(blocks, 0, dim)
+    lengths = blocks.shape
+    return blocks.reshape(*lengths[:dim], lengths[dim] * lengths[dim + 1], *lengths[dim + 2 :])
 
 
 def send_rows(parts):
@@ -197,7 +208,17 @@
     outs = []
     for part in new_state:
         pieces = part.astype(bf16).reshape(experts_here, share, width)
-        spread = lax.all_to_all(pieces, "expert", split_axis=0, concat_axis=0, tiled=True)
+        count_2, here = (lax.axis_size("expert"), lax.axis_index("expert"))
+        blocks = split_up(pieces, 0, count_2)
+        whole = blocks
+        for turn in range(1, count_2):
+            target, source_2 = ((here + turn) % count_2, (here - turn) % count_2)
+            sent = lax.dynamic_index_in_dim(blocks, target, 0)
+            other = lax.ppermute(
+                sent, "expert", [(i, (i + turn) % count_2) for i in range(count_2)]
+            )
+            whole = lax.dynamic_update_slice_in_dim(whole, other, source_2, axis=0)
+        spread = in_order(whole, 0)
         homed = lax.all_to_all(spread[partner], "expert", split_axis=0, concat_axis=0, tiled=True)
         outs.append(homed.reshape(weights.shape))
     return (mixed, token_grad, *outs)

time: 466 us -> 451 us (0.968)
  waiting for transfers between devices: 331 us -> 239 us
  starting transfers between devices: 31.2 us -> 90 us
  local copies, waits for them, and re-layouts: 28.5 us -> 43.6 us
    all_to_all x3 -> x0, waiting for transfers between devices: 95.4 us -> none  [shards_dense(): lax.all_to_all(pieces, 'expert', split_axis=0, concat_axis=0, tiled=True)]
    ppermute x0 -> x45, starting transfers between devices: none -> 68.2 us  [shards_dense(): lax.ppermute(sent, 'expert', [(i, (i + turn) % count_2) for i in range(co...]
    ppermute x0 -> x45, waiting for transfers between devices: none -> 49.7 us  [shards_dense(): lax.ppermute(sent, 'expert', [(i, (i + turn) % count_2) for i in range(co...]
    all_to_all x3, waiting for transfers between devices: 93.4 us -> 60.3 us  [shards_dense(): lax.all_to_all(spread[partner], 'expert', split_axis=0, concat_axis=0, ti...]
    all_to_all x3 -> x0, starting transfers between devices: 16.1 us -> none  [shards_dense(): lax.all_to_all(pieces, 'expert', split_axis=0, concat_axis=0, tiled=True)]
    dynamic_update_slice x0 -> x45, local copies, waits for them, and re-layouts: none -> 14 us  [shards_dense(): whole = lax.dynamic_update_slice_in_dim(whole, other, source_2, axis=0)]
    reduce_scatter x1, waiting for transfers between devices: 25.7 us -> 13 us  [shards_dense(): lax.psum_scatter(partial, 'dp', scatter_dimension=0, tiled=True).astype(f32)]
    all_to_all x3, starting transfers between devices: 14.9 us -> 21.3 us  [shards_dense(): lax.all_to_all(spread[partner], 'expert', split_axis=0, concat_axis=0, ti...]
  transfers between devices with their start and end apart: 12 -> 54, of which waited for: 10 -> 16; matrix products, arithmetic and copies ran while one was open for 10% -> 15% of each run, Pallas kernels for 0% -> 0%
where the time goes in v1:
time: 451 us; the launch traced here: 448 us
  waiting for transfers between devices  239 us (53%)
  starting transfers between devices  90 us (20%)
  local copies, waits for them, and re-layouts  43.6 us (10%)
  matrix products  35.1 us (8%)
  blocking collectives  16 us (4%)
  between operations  15.4 us (3%)
  other arithmetic  8.59 us (2%)
    ppermute x45, starting transfers between devices, shards_dense(): lax.ppermute(sent, 'expert', [(i, (i + turn) % count_2) for i in range(co...  68.2 us
    all_to_all x3, waiting for transfers between devices, shards_dense(): lax.all_to_all(spread[partner], 'expert', split_axis=0, concat_axis=0, ti...  60.3 us
    all_gather x1, waiting for transfers between devices, shards_dense(): x_rows = lax.all_gather(tokens, 'expert', axis=0, tiled=True)  53.2 us
    ppermute x45, waiting for transfers between devices, shards_dense(): lax.ppermute(sent, 'expert', [(i, (i + turn) % count_2) for i in range(co...  49.7 us
    all_gather x1, waiting for transfers between devices, shards_dense(): cot_rows = lax.all_gather(cotangent, 'expert', axis=0, tiled=True)  42.5 us
    all_to_all x3, starting transfers between devices, shards_dense(): lax.all_to_all(spread[partner], 'expert', split_axis=0, concat_axis=0, ti...  21.3 us
    all_gather x1, waiting for transfers between devices, shards_dense(): gathered = lax.all_gather(w_flat, 'dp', axis=0, tiled=True)  19.2 us
    all_gather x1, blocking collectives, shards_dense(): gate_all = lax.all_gather(gate_table, 'expert', axis=0)  16 us
  transfers between devices with their start and end apart: 54, of which 16 were waited for; matrix products, arithmetic and copies ran while one was open for 15% of the time, Pallas kernels for 0%

profile of v1, /device:TPU:15, one launch (start us, length us, event | category | flops | bytes accessed | tf_op | source)
XLA Modules:
  0.0 447.9 jit_solution(9371415144126121954)
XLA Ops:
  11.2 16.0 %all-gather = f32[256,128]{1,0:T(8,128)S(1)} all-gather(f32[16,128]{1,0:T(8,128)S(1)} %bitcast.127), channel_id=2, replica_groups=mesh['dp'=2,'expert'=16] {'expert'}, dimensions={0}, use_global_device_ids=true | all-gather | bytes 139264 | tf_op jit(solution)/shard_map/all_gather | solution.py:178
  27.2 19.2 %all-gather.7.cloned.1.call-done = bf16[1024,1152]{0,1:T(8,128)(2,1)} async-done(((bf16[512,1152]{0,1:T(8,128)(2,1)}), bf16[1024,1152]{0,1:T(8,128)(2,1)}) %all-gather.7.cloned.1.call-update) | async-done | bytes 2359312 | tf_op jit(solution)/shard_map/all_gather | solution.py:175
  46.4 53.2 %all-gather.5.cloned.1.call-done = bf16[2048,1024]{1,0:T(8,128)(2,1)} async-done(((bf16[128,1024]{1,0:T(8,128)(2,1)}), bf16[2048,1024]{1,0:T(8,128)(2,1)}) %all-gather.5.cloned.1.call-update) | async-done | bytes 4194320 | tf_op jit(solution)/shard_map/all_gather | solution.py:176
  99.6 8.7 %fusion.14 = f32[2048,768]{0,1:T(8,128)} fusion(bf16[2048,1024]{1,0:T(8,128)(2,1)} %all-gather.5.cloned.1.call-done, bf16[1024,1152]{0,1:T(8,128)(2,1)} %all-gather.7.cloned.1.call-done), kind=kOutput, calls=%fused_computation.32 | convolution fusion | flops 3221225472 | bytes 12058624 | tf_op jit(solution)/shard_map/dot_general | solution.py:183
  108.3 42.5 %all-gather.9.cloned.1.call-done = bf16[2048,1024]{1,0:T(8,128)(2,1)} async-done(((bf16[128,1024]{1,0:T(8,128)(2,1)}), bf16[2048,1024]{1,0:T(8,128)(2,1)}) %all-gather.9.cloned.1.call-update) | async-done | bytes 4194320 | tf_op jit(solution)/shard_map/all_gather | solution.py:177
  150.8 7.2 %multiply_convert_fusion.3 = (bf16[2048,384]{0,1:T(8,128)(2,1)S(1)}, bf16[2048,384]{0,1:T(8,128)(2,1)S(1)}, bf16[2048,384]{0,1:T(8,128)(2,1)S(1)}) fusion(f32[2048,768]{0,1:T(8,128)} %fusion.14, bf16[1024,1152]{0,1:T(8,128)(2,1)S(1)} %copy-done.33, bf16[2048,1024]{1,0:T(8,128)(2,1)} %all-gather.9.cloned.1.call-done, f32[2048]{0:T(1024)S(1)} %bitcast.128), kind=kOutput, calls=%fused_computation.9 | convolution fusion | flops 1628700672 | bytes 15998976 | tf_op jit(solution)/shard_map/dot_general | solution.py:194
  162.0 3.4 fusion.10
  167.3 5.8 %multiply_convert_fusion.1 = bf16[2048,1024]{1,0:T(8,128)(2,1)} fusion(bf16[2048,384]{0,1:T(8,128)(2,1)} %copy-done.35, f32[2048]{0:T(1024)S(1)} %bitcast.130, bf16[1024,1152]{0,1:T(8,128)(2,1)S(1)} %copy-done.33), kind=kOutput, calls=%fused_computation.4 | convolution fusion | flops 1614807040 | bytes 6561792 | tf_op jit(solution)/shard_map/dot_general | solution.py:189
  179.0 7.9 %convolution_convert_fusion = bf16[2048,1024]{1,0:T(8,128)(2,1)} fusion(bf16[2048,384]{0,1:T(8,128)(2,1)} %copy-done.37, bf16[2048,384]{0,1:T(8,128)(2,1)} %copy-done.36, bf16[1024,1152]{0,1:T(8,128)(2,1)} %all-gather.7.cloned.1.call-done), kind=kOutput, calls=%fused_computation.5 | convolution fusion | flops 3229614080 | bytes 8912896 | tf_op jit(solution)/shard_map/dot_general | solution.py:202
  187.0 13.0 %reduce-scatter.8.cloned.1.call-done = bf16[512,1152]{0,1:T(8,128)(2,1)} async-done(((bf16[1024,1152]{0,1:T(8,128)(2,1)}), bf16[512,1152]{0,1:T(8,128)(2,1)}) %reduce-scatter.8.cloned.1.call-update) | async-done | bytes 1179664 | tf_op jit(solution)/shard_map/reduce_scatter | solution.py:201
  200.0 6.6 %fusion.16 = (bf16[512,1152]{0,1:T(8,128)(2,1)}, bf16[512,1152]{0,1:T(8,128)(2,1)}, bf16[512,1152]{0,1:T(8,128)(2,1)}) fusion(bf16[512,1152]{0,1:T(8,128)(2,1)} %reduce-scatter.8.cloned.1.call-done, f32[1,512,3,384]{1,3,2,0:T(8,128)S(1)} %copy-done.1, f32[1,512,3,384]{1,3,2,0:T(8,128)} %copy.78, bf16[1,512,3,384]{1,3,2,0:T(8,128)(2,1)S(1)} %copy-done), kind=kLoop, calls=%fused_computation.34 | loop fusion | flops 10616832 | bytes 10616832 | tf_op jit(solution)/shard_map/convert_element_type | solution.py:210
  213.4 2.9 collective-permute-start.4
  240.7 5.0 %collective-permute-start.15 = (bf16[1,1,32,1152]{3,2,0,1:T(8,128)(2,1)}, bf16[1,1,32,1152]{3,2,0,1:T(8,128)(2,1)}, u32[]{:S(2)}, u32[]{:S(2)}) collective-permute-start(bf16[1,1,32,1152]{3,2,0,1:T(8,128)(2,1)} %get-tuple-element.50), channel_id=1, source_target_pairs={{0,1},{1,2},{2,3},{3,4},{4,5},{5,6},{6,7},{7,8},{8,9},{9,10},{10,1... | collective-permute-start | bytes 221192 | tf_op jit(solution)/shard_map/ppermute | solution.py:217
  249.0 5.0 %collective-permute-done.13 = bf16[1,1,32,1152]{3,2,0,1:T(8,128)(2,1)S(1)} collective-permute-done((bf16[1,1,32,1152]{3,2,0,1:T(8,128)(2,1)S(1)}, bf16[1,1,32,1152]{3,2,0,1:T(8,128)(2,1)S(1)}, u32[]{:S(2)}, u32[]{:S(2)}) %collective-permute-start.13) | collective-permute-done | bytes 73760 | tf_op jit(solution)/shard_map/ppermute | solution.py:217
  258.5 5.7 %all-to-all-start = ((bf16[16,32,1152]{2,1,0:T(8,128)(2,1)}), bf16[16,32,1152]{2,1,0:T(8,128)(2,1)S(1)}, u32[]{:S(2)}, u32[]{:S(2)}) async-start(bf16[16,32,1152]{2,1,0:T(8,128)(2,1)} %gather_fusion), calls=%async_computation.3 | async-start | bytes 2359296 | tf_op jit(solution)/shard_map/all_to_all | solution.py:222
  273.5 3.0 collective-permute-start.24
  277.5 32.2 %collective-permute-done.20 = bf16[1,1,32,1152]{3,2,0,1:T(8,128)(2,1)S(1)} collective-permute-done((bf16[1,1,32,1152]{3,2,0,1:T(8,128)(2,1)}, bf16[1,1,32,1152]{3,2,0,1:T(8,128)(2,1)S(1)}, u32[]{:S(2)}, u32[]{:S(2)}) %collective-permute-start.20) | collective-permute-done | bytes 73760 | tf_op jit(solution)/shard_map/ppermute | solution.py:217
  334.0 5.7 %collective-permute-done.35 = bf16[1,1,32,1152]{3,2,0,1:T(8,128)(2,1)S(1)} collective-permute-done((bf16[1,1,32,1152]{3,2,0,1:T(8,128)(2,1)S(1)}, bf16[1,1,32,1152]{3,2,0,1:T(8,128)(2,1)S(1)}, u32[]{:S(2)}, u32[]{:S(2)}) %collective-permute-start.35) | collective-permute-done | bytes 73760 | tf_op jit(solution)/shard_map/ppermute | solution.py:217
  339.7 4.2 collective-permute-start.40
  344.4 3.1 collective-permute-start.43
  350.8 10.3 %all-to-all-start.1 = ((bf16[16,32,1152]{2,1,0:T(8,128)(2,1)}), bf16[16,32,1152]{2,1,0:T(8,128)(2,1)S(1)}, u32[]{:S(2)}, u32[]{:S(2)}) async-start(bf16[16,32,1152]{2,1,0:T(8,128)(2,1)} %gather_fusion.1), calls=%async_computation.4 | async-start | bytes 2359296 | tf_op jit(solution)/shard_map/all_to_all | solution.py:222
  367.4 36.1 %all-to-all-done.1 = bf16[16,32,1152]{2,1,0:T(8,128)(2,1)S(1)} async-done(((bf16[16,32,1152]{2,1,0:T(8,128)(2,1)}), bf16[16,32,1152]{2,1,0:T(8,128)(2,1)S(1)}, u32[]{:S(2)}, u32[]{:S(2)}) %all-to-all-start.1) | async-done | bytes 1179680 | tf_op jit(solution)/shard_map/all_to_all | solution.py:222
  404.5 5.3 %all-to-all-start.2 = ((bf16[16,32,1152]{2,1,0:T(8,128)(2,1)}), bf16[16,32,1152]{2,1,0:T(8,128)(2,1)}, u32[]{:S(2)}, u32[]{:S(2)}) async-start(bf16[16,32,1152]{2,1,0:T(8,128)(2,1)} %gather_fusion.2), calls=%async_computation.5 | async-start | bytes 2359296 | tf_op jit(solution)/shard_map/all_to_all | solution.py:222
  413.5 24.2 %all-to-all-done.2 = bf16[16,32,1152]{2,1,0:T(8,128)(2,1)} async-done(((bf16[16,32,1152]{2,1,0:T(8,128)(2,1)}), bf16[16,32,1152]{2,1,0:T(8,128)(2,1)}, u32[]{:S(2)}, u32[]{:S(2)}) %all-to-all-start.2) | async-done | bytes 1179680 | tf_op jit(solution)/shard_map/all_to_all | solution.py:222
  (244 shorter events, 106.2 us)
Async XLA Ops:
  7.2 39.2 %all-gather.7.cloned.1.call-start = ((), (), s32[]{:S(2)}) async-start(), calls=%async_computation.7 | async-start | bytes 3538944 | tf_op jit(solution)/shard_map/all_gather | solution.py:175
  9.6 90.0 %all-gather.5.cloned.1.call-start = ((), (), s32[]{:S(2)}) async-start(), calls=%async_computation.6 | async-start | bytes 4456448 | tf_op jit(solution)/shard_map/all_gather | solution.py:176
  10.4 140.5 %all-gather.9.cloned.1.call-start = ((), (), s32[]{:S(2)}) async-start(), calls=%async_computation.9 | async-start | bytes 4456448 | tf_op jit(solution)/shard_map/all_gather | solution.py:177
  11.1 188.9 %reduce-scatter.8.cloned.1.call-start = ((), (), s32[]{:S(2)}) async-start(), calls=%async_computation.11 | async-start | bytes 3538944 | tf_op jit(solution)/shard_map/reduce_scatter | solution.py:201
  167.1 274.0 %reduce-scatter.4.cloned.1.call-start = ((), (), s32[]{:S(2)}) async-start(), calls=%async_computation.8 | async-start | bytes 4456448 | tf_op jit(solution)/shard_map/reduce_scatter | solution.py:190
  173.1 268.0 %reduce-scatter.6.cloned.1.call-start = ((), (), s32[]{:S(2)}) async-start(), calls=%async_computation.10 | async-start | bytes 4456448 | tf_op jit(solution)/shard_map/reduce_scatter | solution.py:203
  240.7 23.7 %collective-permute-start.15 = (bf16[1,1,32,1152]{3,2,0,1:T(8,128)(2,1)}, bf16[1,1,32,1152]{3,2,0,1:T(8,128)(2,1)}, u32[]{:S(2)}, u32[]{:S(2)}) collective-permute-start(bf16[1,1,32,1152]{3,2,0,1:T(8,128)(2,1)} %get-tuple-element.50), channel_id=1, source_target_pairs={{0,1},{1,2},{2,3},{3,4},{4,5},{5,6},{6,7},{7,8},{8,9},{9,10},{10,1... | collective-permute-start | bytes 221192 | tf_op jit(solution)/shard_map/ppermute | solution.py:217
  245.7 21.7 %collective-permute-start.16 = (bf16[1,1,32,1152]{3,2,0,1:T(8,128)(2,1)}, bf16[1,1,32,1152]{3,2,0,1:T(8,128)(2,1)}, u32[]{:S(2)}, u32[]{:S(2)}) collective-permute-start(bf16[1,1,32,1152]{3,2,0,1:T(8,128)(2,1)} %get-tuple-element.49), channel_id=1, source_target_pairs={{0,2},{1,3},{2,4},{3,5},{4,6},{5,7},{6,8},{7,9},{8,10},{9,11},{10,... | collective-permute-start | bytes 221192 | tf_op jit(solution)/shard_map/ppermute | solution.py:217
  249.0 20.2 %collective-permute-start.17 = (bf16[1,1,32,1152]{3,2,0,1:T(8,128)(2,1)}, bf16[1,1,32,1152]{3,2,0,1:T(8,128)(2,1)}, u32[]{:S(2)}, u32[]{:S(2)}) collective-permute-start(bf16[1,1,32,1152]{3,2,0,1:T(8,128)(2,1)} %get-tuple-element.48), channel_id=1, source_target_pairs={{0,3},{1,4},{2,5},{3,6},{4,7},{5,8},{6,9},{7,10},{8,11},{9,12},{10... | collective-permute-start | bytes 221192 | tf_op jit(solution)/shard_map/ppermute | solution.py:217
  254.0 18.2 %collective-permute-start.18 = (bf16[1,1,32,1152]{3,2,0,1:T(8,128)(2,1)}, bf16[1,1,32,1152]{3,2,0,1:T(8,128)(2,1)}, u32[]{:S(2)}, u32[]{:S(2)}) collective-permute-start(bf16[1,1,32,1152]{3,2,0,1:T(8,128)(2,1)} %get-tuple-element.47), channel_id=1, source_target_pairs={{0,4},{1,5},{2,6},{3,7},{4,8},{5,9},{6,10},{7,11},{8,12},{9,13},{1... | collective-permute-start | bytes 221192 | tf_op jit(solution)/shard_map/ppermute | solution.py:217
  256.0 17.6 %collective-permute-start.19 = (bf16[1,1,32,1152]{3,2,0,1:T(8,128)(2,1)}, bf16[1,1,32,1152]{3,2,0,1:T(8,128)(2,1)}, u32[]{:S(2)}, u32[]{:S(2)}) collective-permute-start(bf16[1,1,32,1152]{3,2,0,1:T(8,128)(2,1)} %get-tuple-element.46), channel_id=1, source_target_pairs={{0,5},{1,6},{2,7},{3,8},{4,9},{5,10},{6,11},{7,12},{8,13},{9,14},{... | collective-permute-start | bytes 221192 | tf_op jit(solution)/shard_map/ppermute | solution.py:217
  258.5 92.3 %all-to-all-start = ((bf16[16,32,1152]{2,1,0:T(8,128)(2,1)}), bf16[16,32,1152]{2,1,0:T(8,128)(2,1)S(1)}, u32[]{:S(2)}, u32[]{:S(2)}) async-start(bf16[16,32,1152]{2,1,0:T(8,128)(2,1)} %gather_fusion), calls=%async_computation.3 | async-start | bytes 2359296 | tf_op jit(solution)/shard_map/all_to_all | solution.py:222
  264.3 45.3 %collective-permute-start.20 = (bf16[1,1,32,1152]{3,2,0,1:T(8,128)(2,1)}, bf16[1,1,32,1152]{3,2,0,1:T(8,128)(2,1)S(1)}, u32[]{:S(2)}, u32[]{:S(2)}) collective-permute-start(bf16[1,1,32,1152]{3,2,0,1:T(8,128)(2,1)} %get-tuple-element.45), channel_id=1, source_target_pairs={{0,6},{1,7},{2,8},{3,9},{4,10},{5,11},{6,12},{7,13},{8,14},{9,15},... | collective-permute-start | bytes 221192 | tf_op jit(solution)/shard_map/ppermute | solution.py:217
  267.4 43.8 %collective-permute-start.21 = (bf16[1,1,32,1152]{3,2,0,1:T(8,128)(2,1)}, bf16[1,1,32,1152]{3,2,0,1:T(8,128)(2,1)S(1)}, u32[]{:S(2)}, u32[]{:S(2)}) collective-permute-start(bf16[1,1,32,1152]{3,2,0,1:T(8,128)(2,1)} %get-tuple-element.44), channel_id=1, source_target_pairs={{0,7},{1,8},{2,9},{3,10},{4,11},{5,12},{6,13},{7,14},{8,15},{9,0},... | collective-permute-start | bytes 221192 | tf_op jit(solution)/shard_map/ppermute | solution.py:217
  269.2 43.6 %collective-permute-start.22 = (bf16[1,1,32,1152]{3,2,0,1:T(8,128)(2,1)}, bf16[1,1,32,1152]{3,2,0,1:T(8,128)(2,1)S(1)}, u32[]{:S(2)}, u32[]{:S(2)}) collective-permute-start(bf16[1,1,32,1152]{3,2,0,1:T(8,128)(2,1)} %get-tuple-element.43), channel_id=1, source_target_pairs={{0,8},{1,9},{2,10},{3,11},{4,12},{5,13},{6,14},{7,15},{8,0},{9,1},... | collective-permute-start | bytes 221192 | tf_op jit(solution)/shard_map/ppermute | solution.py:217
  272.3 43.2 %collective-permute-start.23 = (bf16[1,1,32,1152]{3,2,0,1:T(8,128)(2,1)}, bf16[1,1,32,1152]{3,2,0,1:T(8,128)(2,1)S(1)}, u32[]{:S(2)}, u32[]{:S(2)}) collective-permute-start(bf16[1,1,32,1152]{3,2,0,1:T(8,128)(2,1)} %get-tuple-element.42), channel_id=1, source_target_pairs={{0,9},{1,10},{2,11},{3,12},{4,13},{5,14},{6,15},{7,0},{8,1},{9,2},... | collective-permute-start | bytes 221192 | tf_op jit(solution)/shard_map/ppermute | solution.py:217
  273.5 44.7 %collective-permute-start.24 = (bf16[1,1,32,1152]{3,2,0,1:T(8,128)(2,1)}, bf16[1,1,32,1152]{3,2,0,1:T(8,128)(2,1)S(1)}, u32[]{:S(2)}, u32[]{:S(2)}) collective-permute-start(bf16[1,1,32,1152]{3,2,0,1:T(8,128)(2,1)} %get-tuple-element.41), channel_id=1, source_target_pairs={{0,10},{1,11},{2,12},{3,13},{4,14},{5,15},{6,0},{7,1},{8,2},{9,3},... | collective-permute-start | bytes 221192 | tf_op jit(solution)/shard_map/ppermute | solution.py:217
  339.7 21.5 %collective-permute-start.40 = (bf16[1,1,32,1152]{3,2,0,1:T(8,128)(2,1)}, bf16[1,1,32,1152]{3,2,0,1:T(8,128)(2,1)}, u32[]{:S(2)}, u32[]{:S(2)}) collective-permute-start(bf16[1,1,32,1152]{3,2,0,1:T(8,128)(2,1)} %get-tuple-element.25), channel_id=1, source_target_pairs={{0,11},{1,12},{2,13},{3,14},{4,15},{5,0},{6,1},{7,2},{8,3},{9,4},{... | collective-permute-start | bytes 221192 | tf_op jit(solution)/shard_map/ppermute | solution.py:217
  343.9 18.1 %collective-permute-start.41 = (bf16[1,1,32,1152]{3,2,0,1:T(8,128)(2,1)}, bf16[1,1,32,1152]{3,2,0,1:T(8,128)(2,1)}, u32[]{:S(2)}, u32[]{:S(2)}) collective-permute-start(bf16[1,1,32,1152]{3,2,0,1:T(8,128)(2,1)} %get-tuple-element.24), channel_id=1, source_target_pairs={{0,12},{1,13},{2,14},{3,15},{4,0},{5,1},{6,2},{7,3},{8,4},{9,5},{1... | collective-permute-start | bytes 221192 | tf_op jit(solution)/shard_map/ppermute | solution.py:217
  344.3 18.6 %collective-permute-start.42 = (bf16[1,1,32,1152]{3,2,0,1:T(8,128)(2,1)}, bf16[1,1,32,1152]{3,2,0,1:T(8,128)(2,1)}, u32[]{:S(2)}, u32[]{:S(2)}) collective-permute-start(bf16[1,1,32,1152]{3,2,0,1:T(8,128)(2,1)} %get-tuple-element.23), channel_id=1, source_target_pairs={{0,13},{1,14},{2,15},{3,0},{4,1},{5,2},{6,3},{7,4},{8,5},{9,6},{10... | collective-permute-start | bytes 221192 | tf_op jit(solution)/shard_map/ppermute | solution.py:217
  344.4 19.5 %collective-permute-start.43 = (bf16[1,1,32,1152]{3,2,0,1:T(8,128)(2,1)}, bf16[1,1,32,1152]{3,2,0,1:T(8,128)(2,1)}, u32[]{:S(2)}, u32[]{:S(2)}) collective-permute-start(bf16[1,1,32,1152]{3,2,0,1:T(8,128)(2,1)} %get-tuple-element.22), channel_id=1, source_target_pairs={{0,14},{1,15},{2,0},{3,1},{4,2},{5,3},{6,4},{7,5},{8,6},{9,7},{10,... | collective-permute-start | bytes 221192 | tf_op jit(solution)/shard_map/ppermute | solution.py:217
  347.4 17.4 %collective-permute-start.44 = (bf16[1,1,32,1152]{3,2,0,1:T(8,128)(2,1)}, bf16[1,1,32,1152]{3,2,0,1:T(8,128)(2,1)}, u32[]{:S(2)}, u32[]{:S(2)}) collective-permute-start(bf16[1,1,32,1152]{3,2,0,1:T(8,128)(2,1)} %get-tuple-element.21), channel_id=1, source_target_pairs={{0,15},{1,0},{2,1},{3,2},{4,3},{5,4},{6,5},{7,6},{8,7},{9,8},{10,9... | collective-permute-start | bytes 221192 | tf_op jit(solution)/shard_map/ppermute | solution.py:217
  350.8 52.6 %all-to-all-start.1 = ((bf16[16,32,1152]{2,1,0:T(8,128)(2,1)}), bf16[16,32,1152]{2,1,0:T(8,128)(2,1)S(1)}, u32[]{:S(2)}, u32[]{:S(2)}) async-start(bf16[16,32,1152]{2,1,0:T(8,128)(2,1)} %gather_fusion.1), calls=%async_computation.4 | async-start | bytes 2359296 | tf_op jit(solution)/shard_map/all_to_all | solution.py:222
  404.5 33.2 %all-to-all-start.2 = ((bf16[16,32,1152]{2,1,0:T(8,128)(2,1)}), bf16[16,32,1152]{2,1,0:T(8,128)(2,1)}, u32[]{:S(2)}, u32[]{:S(2)}) async-start(bf16[16,32,1152]{2,1,0:T(8,128)(2,1)} %gather_fusion.2), calls=%async_computation.5 | async-start | bytes 2359296 | tf_op jit(solution)/shard_map/all_to_all | solution.py:222
  (68 other events, 1313.8 us)
Sparse Core Ops, SparseCore 0:
  10.1 36.2 all-gather.6
  48.6 50.9 all-gather.4
  101.8 49.0 all-gather.8
  167.2 32.7 reduce-scatter.7
  204.7 103.3 reduce-scatter.3
  312.4 89.1 reduce-scatter.5
